TPU v7x, 128 devices: a whole 4x4x4 slice. The times are simulated.
128 devices in a mesh: fsdp: 32 (over x, z, core), tensor: 4 (over y).
Axes of the slice: x: 4, y: 4, z: 4, core: 2. Of those that a mesh axis runs over, the one named last changes fastest.
Arguments:
- tokens: bfloat16 [24576, 8192], P('fsdp'), may hold values from -6 to 6
- weight: bfloat16 [8192, 8192], P('fsdp', 'tensor'), may hold values from -0.0625 to 0.0625
- momentum: float32 [8192, 8192], P('fsdp', 'tensor'), may hold values from -700 to 700
- gradient: bfloat16 [8192, 8192], P('fsdp', 'tensor'), may hold values from -6 to 6
- probes: float32 [32, 8192], P(None, 'tensor'), may hold values from -6 to 6
Outputs:
- activations: float32 [24576, 8192], P('fsdp', 'tensor')
- momentum_out: float32 [8192, 8192], P('fsdp', 'tensor')
- krylov_scaled: float32 [96, 96], replicated
All inputs are finite; a program needn't handle non-finite values.
Results may differ from a plain program's by a relative error of at most 0.0029.
Values may be sent and summed in bfloat16 or wider, within the bound.
A program may use at most 192 MiB of HBM per device.

v0:
```python
import jax
import jax.numpy as jnp
from jax import lax
from jax.sharding import PartitionSpec as P

STEPS = 3
SQUARINGS = 5
highest = lax.Precision.HIGHEST


def hdot(left, right):
    return jnp.dot(left, right, precision=highest, preferred_element_type=jnp.float32)


def hdot_t(left, right):
    return lax.dot_general(
        left, right, (((1,), (1,)), ((), ())), precision=highest, preferred_element_type=jnp.float32
    )


def assemble(diag_blocks, low_factors):
    zero = jnp.zeros_like(diag_blocks[0])
    rows = []
    count = len(diag_blocks)
    for row in range(count):
        blocks = []
        for col in range(count):
            if row == col:
                blocks.append(diag_blocks[row])
            elif row == col + 1:
                blocks.append(low_factors[col].T)
            elif col == row + 1:
                blocks.append(low_factors[row])
            else:
                blocks.append(zero)
        rows.append(jnp.concatenate(blocks, axis=1))
    return jnp.concatenate(rows, axis=0)


def top_value(krylov):
    power = krylov / jnp.max(jnp.abs(krylov))
    for _ in range(SQUARINGS):
        power = hdot(power, power)
        power = power / jnp.max(jnp.abs(power))
    vector = jnp.sum(power, axis=1)
    vector = vector / jnp.sqrt(jnp.sum(vector * vector))
    return jnp.sum(vector * hdot(krylov, vector))


def local(tokens, weight, momentum, gradient, probes):
    moment = 0.9 * momentum + gradient.astype(jnp.float32)
    block = probes
    basis_prev = jnp.zeros_like(probes)
    diag_blocks = []
    low_factors = []
    for step in range(STEPS):
        product, gram = lax.psum((hdot_t(block, moment), hdot_t(block, block)), "tensor")
        low = jnp.linalg.cholesky(gram)
        reduced = jax.scipy.linalg.solve_triangular(low, product, lower=True)
        if step:
            low_factors.append(low)
        diag_part = hdot_t(reduced, reduced)
        if step + 1 < STEPS:
            basis = jax.scipy.linalg.solve_triangular(low, block, lower=True)
            images, diag_mat = lax.psum((hdot(reduced, moment), diag_part), "fsdp")
            residue = images - hdot(diag_mat, basis)
            if step:
                residue = residue - hdot(low.T, basis_prev)
            basis_prev, block = (basis, residue)
        else:
            diag_mat = lax.psum(diag_part, "fsdp")
        diag_blocks.append(0.5 * (diag_mat + diag_mat.T))
    krylov = assemble(diag_blocks, low_factors)
    top = top_value(krylov)
    new_weight = (weight.astype(jnp.float32) - moment / jnp.sqrt(top)).astype(jnp.bfloat16)
    summed = jnp.dot(
        tokens,
        lax.all_gather(new_weight, "fsdp", axis=0, tiled=True),
        preferred_element_type=jnp.float32,
    )
    return (summed, moment, krylov / top)


def solution(mesh):
    return jax.shard_map(
        local,
        mesh=mesh,
        in_specs=(
            P("fsdp", None),
            P("fsdp", "tensor"),
            P("fsdp", "tensor"),
            P("fsdp", "tensor"),
            P(None, "tensor"),
        ),
        out_specs=(P("fsdp", "tensor"), P("fsdp", "tensor"), P()),
        check_vma=False,
    )
```

profile of v0, /device:TPU:1, one launch (start us, length us, event | category | flops | bytes accessed | tf_op | source)
XLA Modules:
  0.0 739.3 jit_solution(580088578509843955)
XLA Ops:
  7.2 0.9 copy-done
  8.1 0.3 fusion.37
  8.5 2.3 convert_add_fusion
  10.8 1.8 convolution_bitcast_fusion.1
  12.6 15.8 %all-reduce.2 = (f32[32,256]{0,1:T(8,128)S(1)}, f32[32,32]{0,1:T(8,128)S(1)}) all-reduce(f32[32,256]{0,1:T(8,128)S(1)} %convolution_bitcast_fusion.1, f32[32,32]{0,1:T(8,128)S(1)} %fusion.37), channel_id=1, replica_groups=mesh['fsdp'=32,'tensor'=4] {'tensor'}, use_global_device_ids=true, to_apply=%region_3.5 | all-reduce | flops 9216 | bytes 73728 | tf_op jit(solution)/shard_map/psum | solution.py:57
  28.4 2.9 cholesky.59
  31.4 0.6 compare_reduce_fusion.2
  32.0 0.7 fusion.17
  32.7 2.4 custom-call.11
  35.4 2.0 fusion.39
  37.7 0.4 fusion.29
  38.1 124.4 %psum.79 = f32[32,32]{1,0:T(8,128)S(1)} all-reduce(f32[32,32]{1,0:T(8,128)S(1)} %fusion.38), channel_id=1, replica_groups=mesh['fsdp'=32,'tensor'=4] {'fsdp'}, use_global_device_ids=true, to_apply=%region_4.7 | all-reduce | flops 1024 | bytes 8192 | tf_op jit(solution)/shard_map/psum | solution.py:65
  162.7 1.3 convolution_subtract_fusion.2
  164.0 0.3 fusion.40
  164.3 1.9 fusion.41
  166.3 11.2 %all-reduce.1 = (f32[32,256]{1,0:T(8,128)S(1)}, f32[32,32]{0,1:T(8,128)S(1)}) all-reduce(f32[32,256]{1,0:T(8,128)S(1)} %fusion.41, f32[32,32]{0,1:T(8,128)S(1)} %fusion.40), channel_id=1, replica_groups=mesh['fsdp'=32,'tensor'=4] {'tensor'}, use_global_device_ids=true, to_apply=%region_7.0 | all-reduce | flops 9216 | bytes 73728 | tf_op jit(solution)/shard_map/psum | solution.py:57
  177.6 2.9 cholesky.70
  180.5 0.6 compare_reduce_fusion.1
  181.2 0.7 select_bitcast_fusion.1
  181.8 2.4 custom-call.13
  184.3 0.4 fusion.23
  185.1 2.0 fusion.43
  187.2 127.2 %psum.83 = f32[32,32]{0,1:T(8,128)S(1)} all-reduce(f32[32,32]{0,1:T(8,128)S(1)} %fusion.42), channel_id=1, replica_groups=mesh['fsdp'=32,'tensor'=4] {'fsdp'}, use_global_device_ids=true, to_apply=%region_8.0 | all-reduce | flops 1024 | bytes 8192 | tf_op jit(solution)/shard_map/psum | solution.py:65
  314.8 101.5 %all-reduce.8.cloned.1.call-done = f32[32,2048]{1,0:T(8,128)} async-done(((f32[32,2048]{1,0:T(8,128)}), f32[32,2048]{1,0:T(8,128)}) %all-reduce.8.cloned.1.call-update) | async-done | bytes 262160 | tf_op jit(solution)/shard_map/psum | solution.py:65
  416.3 1.4 convolution_subtract_fusion.1
  417.7 0.4 convolution_subtract_fusion
  418.1 0.4 fusion.44
  418.4 1.9 fusion.45
  420.4 13.6 %all-reduce = (f32[32,256]{1,0:T(8,128)S(1)}, f32[32,32]{0,1:T(8,128)S(1)}) all-reduce(f32[32,256]{1,0:T(8,128)S(1)} %fusion.45, f32[32,32]{0,1:T(8,128)S(1)} %fusion.44), channel_id=1, replica_groups=mesh['fsdp'=32,'tensor'=4] {'tensor'}, use_global_device_ids=true, to_apply=%region_11.0 | all-reduce | flops 9216 | bytes 73728 | tf_op jit(solution)/shard_map/psum | solution.py:57
  434.1 2.9 cholesky.81
  437.1 0.6 compare_reduce_fusion
  437.7 0.7 select_bitcast_fusion
  438.4 2.4 custom-call.15
  441.2 122.6 %psum.87 = f32[32,32]{0,1:T(8,128)S(1)} all-reduce(f32[32,32]{0,1:T(8,128)S(1)} %fusion.46), channel_id=1, replica_groups=mesh['fsdp'=32,'tensor'=4] {'fsdp'}, use_global_device_ids=true, to_apply=%region_12.0 | all-reduce | flops 1024 | bytes 8192 | tf_op jit(solution)/shard_map/psum | solution.py:71
  564.0 0.7 abs_reduce_fusion.5
  564.7 1.4 abs_reduce_fusion.4
  566.1 1.4 abs_reduce_fusion.3
  567.5 1.4 abs_reduce_fusion.2
  569.0 1.4 abs_reduce_fusion.1
  570.4 1.5 abs_reduce_fusion
  571.9 0.7 divide_reduce_fusion
  572.6 0.6 multiply_reduce_fusion
  573.9 0.9 fusion.1
  575.5 1.3 subtract_convert_fusion
  576.8 1.3 broadcast_divide_fusion
  578.1 112.9 %all-gather.2.cloned.1.call-done = bf16[8192,2048]{1,0:T(8,128)(2,1)} async-done(((bf16[256,2048]{1,0:T(8,128)(2,1)}), bf16[8192,2048]{1,0:T(8,128)(2,1)}) %all-gather.2.cloned.1.call-update) | async-done | bytes 33554448 | tf_op jit(solution)/shard_map/all_gather | solution.py:78
  691.0 35.2 %convolution_bitcast_fusion = f32[768,2048]{0,1:T(8,128)} fusion(bf16[8192,2048]{1,0:T(8,128)(2,1)} %all-gather.2.cloned.1.call-done, bf16[768,8192]{1,0:T(8,128)(2,1)} %param.10), kind=kOutput, calls=%fused_computation | convolution fusion | flops 25769803776 | bytes 52428800 | tf_op jit(solution)/shard_map/dot_general | solution.py:76
  726.1 6.6 copy.38
  (38 shorter events, 2.4 us)
Async XLA Ops:
  7.2 1.0 copy-start
  7.2 155.5 %all-reduce.6.cloned.1.call-start = ((), (), s32[]{:S(2)}) async-start(), calls=%async_computation | async-start | bytes 524288 | tf_op jit(solution)/shard_map/psum | solution.py:65
  10.8 564.7 %copy-start.2 = (f32[256,2048]{1,0:T(8,128)}, f32[256,2048]{1,0:T(8,128)S(1)}, u32[]{:S(2)}) copy-start(f32[256,2048]{1,0:T(8,128)S(1)} %convert_add_fusion) | copy-start | bytes 6291460
  37.5 378.8 %all-reduce.8.cloned.1.call-start = ((), (), s32[]{:S(2)}) async-start(), calls=%async_computation.1 | async-start | bytes 524288 | tf_op jit(solution)/shard_map/psum | solution.py:65
  314.5 376.4 %all-gather.2.cloned.1.call-start = ((), (), s32[]{:S(2)}) async-start(), calls=%async_computation.2 | async-start | bytes 34603008 | tf_op jit(solution)/shard_map/all_gather | solution.py:78
  418.4 157.0 %copy-start.3 = (bf16[256,2048]{1,0:T(8,128)(2,1)S(1)}, bf16[256,2048]{1,0:T(8,128)(2,1)}, u32[]{:S(2)}) copy-start(bf16[256,2048]{1,0:T(8,128)(2,1)} %param.11) | copy-start | bytes 3145732
  726.1 6.6 copy-start.1
Sparse Core Ops, SparseCore 0:
  37.6 105.8 all-reduce.5
  314.7 101.5 all-reduce.7
  576.9 114.0 all-gather.1
where the time goes:
time: 740 us; the launch traced here: 739 us
  blocking collectives  415 us (56%)
  waiting for transfers between devices  214 us (29%)
  matrix products  59.1 us (8%)
  other arithmetic  27 us (4%)
  between operations  15.4 us (2%)
  local copies, waits for them, and re-layouts  8.1 us (1%)
    psum x2, blocking collectives, local(): images, diag_mat = lax.psum((hdot(reduced, moment), diag_part), 'fsdp')  252 us
    psum x1, blocking collectives, local(): diag_mat = lax.psum(diag_part, 'fsdp')  123 us
    all_gather x1, waiting for transfers between devices, local(): lax.all_gather(new_weight, 'fsdp', axis=0, tiled=True)  113 us
    psum x2, waiting for transfers between devices, local(): images, diag_mat = lax.psum((hdot(reduced, moment), diag_part), 'fsdp')  102 us
    psum x3, blocking collectives, local(): lax.psum((hdot_t(block, moment), hdot_t(block, block)), 'tensor')  40.7 us
    dot_general x1, matrix products, local(): jnp.dot(tokens, lax.all_gather(new_weight, 'fsdp', axis=0, tiled=True), p...  35.2 us
    dot_general x11, matrix products, hdot(): jnp.dot(left, right, precision=highest, preferred_element_type=jnp.float32)  15.2 us
  transfers between devices with their start and end apart: 3, of which 2 were waited for; matrix products, arithmetic and copies ran while one was open for 0% of the time, Pallas kernels for 0%

commit v1 on v0

--- a/solution.py
+++ b/solution.py
@@ -75,7 +75,9 @@
     new_weight = (weight.astype(jnp.float32) - moment / jnp.sqrt(top)).astype(jnp.bfloat16)
     summed = jnp.dot(
         tokens,
-        lax.all_gather(new_weight, "fsdp", axis=0, tiled=True),
+        jnp.concatenate(
+            lax.all_to_all(jnp.stack([new_weight] * lax.axis_size("fsdp")), "fsdp", 0, 0), axis=0
+        ),
         preferred_element_type=jnp.float32,
     )
     return (summed, moment, krylov / top)

time: 740 us -> 1190 us (1.61)
  the two profiles are of different devices: /device:TPU:1 before, /device:TPU:36 now
where the time goes in v1:
time: 1190 us
  waiting for transfers between devices  676 us (57%)
  blocking collectives  367 us (31%)
  matrix products  59.1 us (5%)
  starting transfers between devices  29.6 us (2%)
  other arithmetic  26 us (2%)
  local copies, waits for them, and re-layouts  19.1 us (2%)
  between operations  15.7 us (1%)
    all_to_all x1, waiting for transfers between devices, local(): lax.all_to_all(jnp.stack([new_weight] * lax.axis_size('fsdp')), 'fsdp', 0...  547 us
    psum x2, blocking collectives, local(): images, diag_mat = lax.psum((hdot(reduced, moment), diag_part), 'fsdp')  213 us
    psum x2, waiting for transfers between devices, local(): images, diag_mat = lax.psum((hdot(reduced, moment), diag_part), 'fsdp')  129 us
    psum x1, blocking collectives, local(): diag_mat = lax.psum(diag_part, 'fsdp')  101 us
    psum x3, blocking collectives, local(): lax.psum((hdot_t(block, moment), hdot_t(block, block)), 'tensor')  52.9 us
    dot_general x1, matrix products, local(): jnp.dot(tokens, jnp.concatenate(lax.all_to_all(jnp.stack([new_weight] * l...  35.2 us
    all_to_all x1, starting transfers between devices, local(): lax.all_to_all(jnp.stack([new_weight] * lax.axis_size('fsdp')), 'fsdp', 0...  29.5 us
  transfers between devices with their start and end apart: 3, of which 2 were waited for; matrix products, arithmetic and copies ran while one was open for 0% of the time, Pallas kernels for 0%

profile of v1, /device:TPU:36, one launch (start us, length us, event | category | flops | bytes accessed | tf_op | source)
XLA Modules:
  0.0 1193.0 jit_solution(522638907285204725)
XLA Ops:
  7.2 0.9 copy-done
  8.1 0.4 fusion.37
  8.5 2.3 convert_add_fusion
  10.8 1.8 convolution_bitcast_fusion.1
  12.6 18.7 %all-reduce.2 = (f32[32,256]{0,1:T(8,128)S(1)}, f32[32,32]{0,1:T(8,128)S(1)}) all-reduce(f32[32,256]{0,1:T(8,128)S(1)} %convolution_bitcast_fusion.1, f32[32,32]{0,1:T(8,128)S(1)} %fusion.37), channel_id=1, replica_groups=mesh['fsdp'=32,'tensor'=4] {'tensor'}, use_global_device_ids=true, to_apply=%region_3.5 | all-reduce | flops 9216 | bytes 73728 | tf_op jit(solution)/shard_map/psum | solution.py:57
  31.4 2.9 cholesky.59
  34.3 0.6 compare_reduce_fusion.2
  35.0 0.7 fusion.17
  35.6 2.4 custom-call.11
  38.4 2.0 fusion.39
  40.6 0.4 fusion.29
  41.0 100.5 %psum.79 = f32[32,32]{1,0:T(8,128)S(1)} all-reduce(f32[32,32]{1,0:T(8,128)S(1)} %fusion.38), channel_id=1, replica_groups=mesh['fsdp'=32,'tensor'=4] {'fsdp'}, use_global_device_ids=true, to_apply=%region_4.7 | all-reduce | flops 1024 | bytes 8192 | tf_op jit(solution)/shard_map/psum | solution.py:65
  141.6 1.3 convolution_subtract_fusion.2
  142.9 0.3 fusion.40
  143.3 1.9 fusion.41
  145.2 16.8 %all-reduce.1 = (f32[32,256]{1,0:T(8,128)S(1)}, f32[32,32]{0,1:T(8,128)S(1)}) all-reduce(f32[32,256]{1,0:T(8,128)S(1)} %fusion.41, f32[32,32]{0,1:T(8,128)S(1)} %fusion.40), channel_id=1, replica_groups=mesh['fsdp'=32,'tensor'=4] {'tensor'}, use_global_device_ids=true, to_apply=%region_7.0 | all-reduce | flops 9216 | bytes 73728 | tf_op jit(solution)/shard_map/psum | solution.py:57
  162.1 2.9 cholesky.70
  165.1 0.6 compare_reduce_fusion.1
  165.7 0.7 select_bitcast_fusion.1
  166.4 2.4 custom-call.13
  168.8 0.4 fusion.23
  169.6 2.0 fusion.43
  171.7 112.9 %psum.83 = f32[32,32]{0,1:T(8,128)S(1)} all-reduce(f32[32,32]{0,1:T(8,128)S(1)} %fusion.42), channel_id=1, replica_groups=mesh['fsdp'=32,'tensor'=4] {'fsdp'}, use_global_device_ids=true, to_apply=%region_8.0 | all-reduce | flops 1024 | bytes 8192 | tf_op jit(solution)/shard_map/psum | solution.py:65
  284.7 129.3 %all-reduce.8.cloned.1.call-done = f32[32,2048]{1,0:T(8,128)} async-done(((f32[32,2048]{1,0:T(8,128)}), f32[32,2048]{1,0:T(8,128)}) %all-reduce.8.cloned.1.call-update) | async-done | bytes 262160 | tf_op jit(solution)/shard_map/psum | solution.py:65
  414.0 1.4 convolution_subtract_fusion.1
  415.4 0.4 convolution_subtract_fusion
  416.2 1.9 fusion.45
  418.1 17.4 %all-reduce = (f32[32,256]{1,0:T(8,128)S(1)}, f32[32,32]{0,1:T(8,128)S(1)}) all-reduce(f32[32,256]{1,0:T(8,128)S(1)} %fusion.45, f32[32,32]{0,1:T(8,128)S(1)} %fusion.44), channel_id=1, replica_groups=mesh['fsdp'=32,'tensor'=4] {'tensor'}, use_global_device_ids=true, to_apply=%region_11.0 | all-reduce | flops 9216 | bytes 73728 | tf_op jit(solution)/shard_map/psum | solution.py:57
  435.6 2.9 cholesky.81
  438.6 0.6 compare_reduce_fusion
  439.2 0.7 select_bitcast_fusion
  439.9 2.4 custom-call.15
  442.7 101.2 %psum.87 = f32[32,32]{0,1:T(8,128)S(1)} all-reduce(f32[32,32]{0,1:T(8,128)S(1)} %fusion.46), channel_id=1, replica_groups=mesh['fsdp'=32,'tensor'=4] {'fsdp'}, use_global_device_ids=true, to_apply=%region_12.0 | all-reduce | flops 1024 | bytes 8192 | tf_op jit(solution)/shard_map/psum | solution.py:71
  544.1 0.7 abs_reduce_fusion.5
  544.8 1.4 abs_reduce_fusion.4
  546.2 1.4 abs_reduce_fusion.3
  547.7 1.4 abs_reduce_fusion.2
  549.1 1.4 abs_reduce_fusion.1
  550.5 1.5 abs_reduce_fusion
  552.1 0.7 divide_reduce_fusion
  552.7 0.6 multiply_reduce_fusion
  554.0 0.8 fusion.1
  555.9 11.0 stack.2
  566.9 29.5 %all-to-all-start = ((bf16[32,256,2048]{2,1,0:T(8,128)(2,1)}), bf16[32,256,2048]{2,1,0:T(8,128)(2,1)}, u32[]{:S(2)}, u32[]{:S(2)}) async-start(bf16[32,256,2048]{2,1,0:T(8,128)(2,1)} %stack.2), calls=%async_computation | async-start | bytes 67108864 | tf_op jit(solution)/shard_map/all_to_all | solution.py:79
  596.4 1.3 broadcast_divide_fusion
  597.7 546.7 %all-to-all-done = bf16[32,256,2048]{2,1,0:T(8,128)(2,1)} async-done(((bf16[32,256,2048]{2,1,0:T(8,128)(2,1)}), bf16[32,256,2048]{2,1,0:T(8,128)(2,1)}, u32[]{:S(2)}, u32[]{:S(2)}) %all-to-all-start) | async-done | bytes 33554464 | tf_op jit(solution)/shard_map/all_to_all | solution.py:79
  1144.4 35.2 %convolution_bitcast_fusion = f32[768,2048]{0,1:T(8,128)} fusion(bf16[8192,2048]{1,0:T(8,128)(2,1)} %bitcast.21, bf16[768,8192]{1,0:T(8,128)(2,1)} %param.10), kind=kOutput, calls=%fused_computation | convolution fusion | flops 25769803776 | bytes 52428800 | tf_op jit(solution)/shard_map/dot_general | solution.py:76
  1179.6 6.6 copy.38
  (38 shorter events, 2.8 us)
Async XLA Ops:
  7.2 1.0 copy-start
  7.2 134.4 %all-reduce.6.cloned.1.call-start = ((), (), s32[]{:S(2)}) async-start(), calls=%async_computation.1 | async-start | bytes 524288 | tf_op jit(solution)/shard_map/psum | solution.py:65
  10.8 544.7 %copy-start.2 = (f32[256,2048]{1,0:T(8,128)}, f32[256,2048]{1,0:T(8,128)S(1)}, u32[]{:S(2)}) copy-start(f32[256,2048]{1,0:T(8,128)S(1)} %convert_add_fusion) | copy-start | bytes 6291460
  40.4 373.6 %all-reduce.8.cloned.1.call-start = ((), (), s32[]{:S(2)}) async-start(), calls=%async_computation.2 | async-start | bytes 524288 | tf_op jit(solution)/shard_map/psum | solution.py:65
  416.2 139.3 %copy-start.3 = (bf16[256,2048]{1,0:T(8,128)(2,1)S(1)}, bf16[256,2048]{1,0:T(8,128)(2,1)}, u32[]{:S(2)}) copy-start(bf16[256,2048]{1,0:T(8,128)(2,1)} %param.11) | copy-start | bytes 3145732
  566.9 577.5 %all-to-all-start = ((bf16[32,256,2048]{2,1,0:T(8,128)(2,1)}), bf16[32,256,2048]{2,1,0:T(8,128)(2,1)}, u32[]{:S(2)}, u32[]{:S(2)}) async-start(bf16[32,256,2048]{2,1,0:T(8,128)(2,1)} %stack.2), calls=%async_computation | async-start | bytes 67108864 | tf_op jit(solution)/shard_map/all_to_all | solution.py:79
  1179.6 6.6 copy-start.1
Sparse Core Ops, SparseCore 0:
  40.5 100.3 all-reduce.5
  284.8 129.1 all-reduce.7
